TPU v7x, 256 devices: a whole 4x4x8 slice. The times are simulated.
256 devices in a mesh: row: 16 (over z_lo, x), col: 16 (over y, z_hi, core).
Axes of the slice: x: 4, y: 4, z: 8 (z_hi: 2, z_lo: 4; z = z_hi * 4 + z_lo), core: 2. Of those that a mesh axis runs over, the one named last changes fastest.
Arguments:
- inverse_block: bfloat16 [10240, 10240], P('row', 'col'), may hold values from -6 to 6
- factor_cols: bfloat16 [10240, 4096], P('row', 'col'), may hold values from -0.078125 to 0.078125
- diag_inverse: float32 [16, 256, 256], P('col', 'row'), may hold values from -6 to 6
- fill_mask: int32 [40, 16], replicated, may hold values from 0 to 1
Outputs:
- inverse_cols: bfloat16 [10240, 4096], P('row', 'col')
- inverse_diag: float32 [16, 256, 256], P('col', 'row')
All inputs are finite; a program needn't handle non-finite values.
Results may differ from a plain program's by a relative error of at most 0.0027.
Values may be sent and summed in bfloat16 or wider, within the bound.
No kernel may reach another device: no remote copies, remote signals or barrier semaphores. Data moves between devices by JAX's collectives and lax.ppermute only.
A program may use at most 64 MiB of HBM per device.

v0:
```python
import jax
import jax.numpy as jnp
from jax import lax
from jax.sharding import PartitionSpec as P


def body(inverse_block, factor_cols, diag_inverse, fill_mask):
    rows_device, cols_device = factor_cols.shape
    nodes_device, diag_rows, block_width = diag_inverse.shape
    block_count, node_count = fill_mask.shape
    row_index = lax.axis_index("row")
    col_index = lax.axis_index("col")
    expanded = jnp.broadcast_to(
        fill_mask[:, None, :], (block_count, block_width, node_count)
    ).reshape(block_count * block_width, node_count)
    local_mask = lax.dynamic_slice(
        expanded, (row_index * rows_device, col_index * nodes_device), (rows_device, nodes_device)
    )
    column_mask = jnp.broadcast_to(
        local_mask[:, :, None], (rows_device, nodes_device, block_width)
    ).reshape(rows_device, cols_device)
    selected = factor_cols * column_mask.astype(jnp.bfloat16)
    gathered_panel = lax.all_gather(selected, "row", axis=0, tiled=True)
    spread = lax.all_to_all(gathered_panel, "col", split_axis=0, concat_axis=1, tiled=True)
    partial_value = jnp.dot(inverse_block, spread, preferred_element_type=jnp.float32)
    summed = lax.psum_scatter(partial_value, "col", scatter_dimension=1, tiled=True)
    inverse_cols = (-summed * column_mask.astype(jnp.float32)).astype(jnp.bfloat16)
    left_side = selected.reshape(rows_device, nodes_device, block_width)
    right_side = inverse_cols.reshape(rows_device, nodes_device, block_width)
    correction = jnp.einsum(
        "isa,isb->sab", left_side, right_side, preferred_element_type=jnp.float32
    )
    shared = lax.psum_scatter(correction, "row", scatter_dimension=1, tiled=True)
    inverse_diag = diag_inverse - shared
    return (inverse_cols, inverse_diag)


def solution(mesh):
    placed = (P("row", "col"), P("row", "col"), P("col", "row", None), P())
    return jax.shard_map(
        body,
        mesh=mesh,
        in_specs=placed,
        out_specs=(P("row", "col"), P("col", "row", None)),
        check_vma=False,
    )
```

profile of v0, /device:TPU:8, one launch (start us, length us, event | category | flops | bytes accessed | tf_op | source)
XLA Modules:
  0.0 491.6 jit_solution(3186827072917401955)
XLA Ops:
  7.2 0.0 copy-start
  7.2 0.0 all-gather.2.cloned.1.call-start
  7.2 0.9 broadcast_in_dim.2
  8.1 0.2 copy.11
  8.4 0.1 convert_reduce_fusion.1
  8.5 1.9 broadcast_multiply_fusion
  10.3 0.0 all-gather.2.cloned.1.call-update
  10.3 0.0 reduce-scatter.3.cloned.1.call-start
  10.4 92.8 %all-gather.2.cloned.1.call-done = bf16[10240,256]{1,0:T(8,128)(2,1)} async-done(((bf16[640,256]{1,0:T(8,128)(2,1)}), bf16[10240,256]{1,0:T(8,128)(2,1)}) %all-gather.2.cloned.1.call-update) | async-done | bytes 5242896 | tf_op jit(solution)/shard_map/all_gather | solution.py:23
  103.2 117.7 %all_to_all.19 = bf16[16,640,256]{2,1,0:T(8,128)(2,1)} all-to-all(bf16[16,640,256]{2,1,0:T(8,128)(2,1)} %bitcast.16), channel_id=1, replica_groups=mesh['row'=16,'col'=16] {'col'}, dimensions={0} | all-to-all | bytes 10485760 | tf_op jit(solution)/shard_map/all_to_all | solution.py:24
  220.9 7.9 %copy.9 = bf16[640,16,256]{0,2,1:T(8,128)(2,1)} copy(bf16[640,16,256]{2,0,1:T(8,128)(2,1)} %bitcast.15) | data formatting | bytes 10485760 | tf_op jit(solution)/shard_map/all_to_all | solution.py:24
  228.8 0.0 copy-done
  228.8 9.7 %convolution_bitcast_fusion = f32[640,4096]{0,1:T(8,128)} fusion(bf16[640,4096]{0,1:T(8,128)(2,1)} %bitcast.17, bf16[640,640]{1,0:T(8,128)(2,1)S(1)} %copy-done), kind=kOutput, calls=%fused_computation | convolution fusion | flops 3355443200 | bytes 16547840 | tf_op jit(solution)/shard_map/dot_general | solution.py:25
  238.5 0.0 reduce-scatter.3.cloned.1.call-update
  238.5 0.0 reduce-scatter.5.cloned.1.call-start
  238.6 0.1 convert_reduce_fusion
  238.7 161.4 %reduce-scatter.3.cloned.1.call-done = f32[640,256]{0,1:T(8,128)} async-done(((f32[640,4096]{0,1:T(8,128)}), f32[640,256]{0,1:T(8,128)}) %reduce-scatter.3.cloned.1.call-update) | async-done | bytes 655376 | tf_op jit(solution)/shard_map/reduce_scatter | solution.py:26
  400.0 1.1 multiply_convert_fusion
  401.2 1.0 convolution_bitcast_fusion.1
  402.2 0.0 reduce-scatter.5.cloned.1.call-update
  402.2 0.9 copy.10
  403.1 80.6 %reduce-scatter.5.cloned.1.call-done = f32[1,16,256]{2,1,0:T(8,128)} async-done(((f32[1,256,256]{2,1,0:T(8,128)}), f32[1,16,256]{2,1,0:T(8,128)}) %reduce-scatter.5.cloned.1.call-update) | async-done | bytes 16400 | tf_op jit(solution)/shard_map/reduce_scatter | solution.py:33
  483.7 0.0 copy-done.2
  483.7 1.3 sub.3
  (3 shorter events, 0.0 us)
Async XLA Ops:
  7.2 221.6 %copy-start = (bf16[640,640]{1,0:T(8,128)(2,1)S(1)}, bf16[640,640]{1,0:T(8,128)(2,1)}, u32[]{:S(2)}) copy-start(bf16[640,640]{1,0:T(8,128)(2,1)} %param.4) | copy-start | bytes 2457604
  7.2 96.0 %all-gather.2.cloned.1.call-start = ((), (), s32[]{:S(2)}) async-start(), calls=%async_computation.3 | async-start | bytes 5570560 | tf_op jit(solution)/shard_map/all_gather | solution.py:23
  10.3 389.7 %reduce-scatter.3.cloned.1.call-start = ((), (), s32[]{:S(2)}) async-start(), calls=%async_computation.4 | async-start | bytes 11141120 | tf_op jit(solution)/shard_map/reduce_scatter | solution.py:26
  238.5 162.7 %copy-start.1 = (bf16[640,256]{1,0:T(8,128)(2,1)S(1)}, bf16[640,256]{1,0:T(8,128)(2,1)}, u32[]{:S(2)}) copy-start(bf16[640,256]{1,0:T(8,128)(2,1)} %broadcast_multiply_fusion) | copy-start | bytes 983044
  238.5 245.2 %copy-start.2 = (f32[1,16,256]{2,1,0:T(8,128)S(1)}, f32[1,16,256]{2,1,0:T(8,128)}, u32[]{:S(2)}) copy-start(f32[1,16,256]{2,1,0:T(8,128)} %param.6) | copy-start | bytes 49156
  238.5 245.2 %reduce-scatter.5.cloned.1.call-start = ((), (), s32[]{:S(2)}) async-start(), calls=%async_computation.5 | async-start | bytes 278528 | tf_op jit(solution)/shard_map/reduce_scatter | solution.py:33
Sparse Core Ops, SparseCore 0:
  10.4 92.7 all-gather.1
  238.7 161.3 reduce-scatter.2
  402.5 81.1 reduce-scatter.4
where the time goes:
time: 492 us
  waiting for transfers between devices  335 us (68%)
  blocking collectives  118 us (24%)
  between operations  13.8 us (3%)
  matrix products  10.7 us (2%)
  local copies, waits for them, and re-layouts  9.88 us (2%)
    reduce_scatter x1, waiting for transfers between devices, body(): lax.psum_scatter(partial_value, 'col', scatter_dimension=1, tiled=True)  161 us
    all_to_all x1, blocking collectives, body(): lax.all_to_all(gathered_panel, 'col', split_axis=0, concat_axis=1, tiled=...  118 us
    all_gather x1, waiting for transfers between devices, body(): gathered_panel = lax.all_gather(selected, 'row', axis=0, tiled=True)  92.8 us
    reduce_scatter x1, waiting for transfers between devices, body(): lax.psum_scatter(correction, 'row', scatter_dimension=1, tiled=True)  80.6 us
  transfers between devices with their start and end apart: 3, of which 3 were waited for; matrix products, arithmetic and copies ran while one was open for 0% of the time, Pallas kernels for 0%

commit v1 on v0

--- a/solution.py
+++ b/solution.py
@@ -20,7 +20,9 @@
         local_mask[:, :, None], (rows_device, nodes_device, block_width)
     ).reshape(rows_device, cols_device)
     selected = factor_cols * column_mask.astype(jnp.bfloat16)
-    gathered_panel = lax.all_gather(selected, "row", axis=0, tiled=True)
+    gathered_panel = jnp.concatenate(
+        lax.all_to_all(jnp.stack([selected] * lax.axis_size("row")), "row", 0, 0), axis=0
+    )
     spread = lax.all_to_all(gathered_panel, "col", split_axis=0, concat_axis=1, tiled=True)
     partial_value = jnp.dot(inverse_block, spread, preferred_element_type=jnp.float32)
     summed = lax.psum_scatter(partial_value, "col", scatter_dimension=1, tiled=True)

time: 492 us -> 518 us (1.053)
  blocking collectives: 118 us -> 201 us
  waiting for transfers between devices: 335 us -> 288 us
  local copies, waits for them, and re-layouts: 9.88 us -> 2.83 us
    all_to_all x0 -> x1, blocking collectives: none -> 125 us  [body(): lax.all_to_all(jnp.stack([selected] * lax.axis_size('row')), 'row', 0, 0)]
    all_gather x1 -> x0, waiting for transfers between devices: 92.8 us -> none  [body(): gathered_panel = lax.all_gather(selected, 'row', axis=0, tiled=True)]
    reduce_scatter x1, waiting for transfers between devices: 161 us -> 207 us  [body(): lax.psum_scatter(partial_value, 'col', scatter_dimension=1, tiled=True)]
    all_to_all x1, blocking collectives: 118 us -> 76.2 us  [body(): lax.all_to_all(gathered_panel, 'col', split_axis=0, concat_axis=1, tiled=...]
    all_to_all x1 -> x0, local copies, waits for them, and re-layouts: 7.86 us -> none  [body(): lax.all_to_all(gathered_panel, 'col', split_axis=0, concat_axis=1, tiled=...]
  transfers between devices with their start and end apart: 3 -> 2, of which waited for: 3 -> 2; matrix products, arithmetic and copies ran while one was open for 0% -> 0% of each run, Pallas kernels for 0% -> 0%
where the time goes in v1:
time: 518 us
  waiting for transfers between devices  288 us (56%)
  blocking collectives  201 us (39%)
  between operations  14.1 us (3%)
  matrix products  8.34 us (2%)
    reduce_scatter x1, waiting for transfers between devices, body(): lax.psum_scatter(partial_value, 'col', scatter_dimension=1, tiled=True)  207 us
    all_to_all x1, blocking collectives, body(): lax.all_to_all(jnp.stack([selected] * lax.axis_size('row')), 'row', 0, 0)  125 us
    reduce_scatter x1, waiting for transfers between devices, body(): lax.psum_scatter(correction, 'row', scatter_dimension=1, tiled=True)  80.6 us
    all_to_all x1, blocking collectives, body(): lax.all_to_all(gathered_panel, 'col', split_axis=0, concat_axis=1, tiled=...  76.2 us
  transfers between devices with their start and end apart: 2, of which 2 were waited for; matrix products, arithmetic and copies ran while one was open for 0% of the time, Pallas kernels for 0%

profile of v1, /device:TPU:8, one launch (start us, length us, event | category | flops | bytes accessed | tf_op | source)
XLA Modules:
  0.0 517.8 jit_solution(9733966588426952832)
XLA Ops:
  7.2 0.0 copy-start
  7.2 0.0 reduce-scatter.3.cloned.1.call-start
  7.2 0.9 broadcast_in_dim.2
  8.1 0.2 copy.10
  8.3 0.1 convert_reduce_fusion.1
  8.4 1.1 broadcast_multiply_fusion
  9.6 0.2 copy.8
  9.8 0.6 stack.2
  10.4 124.8 %all_to_all.21 = bf16[16,640,256]{1,2,0:T(8,128)(2,1)S(1)} all-to-all(bf16[16,640,256]{1,2,0:T(8,128)(2,1)S(1)} %stack.2), channel_id=1, replica_groups=mesh['row'=16,'col'=16] {'row'}, dimensions={0} | all-to-all | bytes 10485760 | tf_op jit(solution)/shard_map/all_to_all | solution.py:24
  135.2 76.2 %all_to_all.22 = bf16[16,640,256]{1,2,0:T(8,128)(2,1)S(1)} all-to-all(bf16[16,640,256]{1,2,0:T(8,128)(2,1)S(1)} %all_to_all.21), channel_id=1, replica_groups=mesh['row'=16,'col'=16] {'col'}, dimensions={0} | all-to-all | bytes 10485760 | tf_op jit(solution)/shard_map/all_to_all | solution.py:26
  211.3 0.0 copy-done
  211.3 7.3 %convolution_bitcast_fusion = f32[640,4096]{0,1:T(8,128)} fusion(bf16[640,4096]{0,1:T(8,128)(2,1)S(1)} %bitcast.15, bf16[640,640]{1,0:T(8,128)(2,1)S(1)} %copy-done), kind=kOutput, calls=%fused_computation | convolution fusion | flops 3355443200 | bytes 16547840 | tf_op jit(solution)/shard_map/dot_general | solution.py:27
  218.7 0.0 copy-start.1
  218.7 0.0 reduce-scatter.3.cloned.1.call-update
  218.7 0.0 reduce-scatter.5.cloned.1.call-start
  218.8 0.1 convert_reduce_fusion
  218.9 207.1 %reduce-scatter.3.cloned.1.call-done = f32[640,256]{0,1:T(8,128)} async-done(((f32[640,4096]{0,1:T(8,128)}), f32[640,256]{0,1:T(8,128)}) %reduce-scatter.3.cloned.1.call-update) | async-done | bytes 655376 | tf_op jit(solution)/shard_map/reduce_scatter | solution.py:28
  426.0 1.1 multiply_convert_fusion
  427.1 1.0 convolution_bitcast_fusion.1
  428.1 0.0 reduce-scatter.5.cloned.1.call-update
  428.2 0.9 copy.9
  429.1 80.6 %reduce-scatter.5.cloned.1.call-done = f32[1,16,256]{2,1,0:T(8,128)} async-done(((f32[1,256,256]{2,1,0:T(8,128)}), f32[1,16,256]{2,1,0:T(8,128)}) %reduce-scatter.5.cloned.1.call-update) | async-done | bytes 16400 | tf_op jit(solution)/shard_map/reduce_scatter | solution.py:35
  509.6 0.0 copy-done.1
  509.6 1.3 sub.3
Async XLA Ops:
  7.2 204.2 %copy-start = (bf16[640,640]{1,0:T(8,128)(2,1)S(1)}, bf16[640,640]{1,0:T(8,128)(2,1)}, u32[]{:S(2)}) copy-start(bf16[640,640]{1,0:T(8,128)(2,1)} %param.4) | copy-start | bytes 2457604
  7.2 418.8 %reduce-scatter.3.cloned.1.call-start = ((), (), s32[]{:S(2)}) async-start(), calls=%async_computation.4 | async-start | bytes 11141120 | tf_op jit(solution)/shard_map/reduce_scatter | solution.py:28
  218.7 290.9 %copy-start.1 = (f32[1,16,256]{2,1,0:T(8,128)S(1)}, f32[1,16,256]{2,1,0:T(8,128)}, u32[]{:S(2)}) copy-start(f32[1,16,256]{2,1,0:T(8,128)} %param.6) | copy-start | bytes 49156
  218.7 290.9 %reduce-scatter.5.cloned.1.call-start = ((), (), s32[]{:S(2)}) async-start(), calls=%async_computation.5 | async-start | bytes 278528 | tf_op jit(solution)/shard_map/reduce_scatter | solution.py:35
Sparse Core Ops, SparseCore 0:
  218.8 207.1 reduce-scatter.2
  428.5 81.1 reduce-scatter.4
